TPU v7x, 256 devices: a whole 4x4x8 slice. The times are simulated.
256 devices in a mesh: row: 16 (over z_lo, x, core), col: 16 (over z_hi, y).
Axes of the slice: x: 4, y: 4, z: 8 (z_hi: 4, z_lo: 2; z = z_hi * 2 + z_lo), core: 2. Of those that a mesh axis runs over, the one named last changes fastest.
Arguments:
- embeddings: bfloat16 [32768, 768], P(('row', 'col')), may hold values from -400 to 400
- tile_list: int32 [16, 16, 32, 2], P('row', 'col'), may hold values from -1 to 15, as said below
- seeds: int32 [32768], P(('row', 'col')), may hold values from 0 to 127
Outputs:
- scores: float32 [32768, 64], P(('row', 'col'))
Inputs may be any that keep to these rules, and one draw needn't show every extreme that they name: tile_list[r, c] lists the tiles of the device at row index r and column index c: a live slot (a, b) stands for the tile of document block r * 16 + a against block b * 16 + c, with a < 16, b < 16 and r * 16 + a <= b * 16 + c. Live slots come first and are distinct, empty slots hold -1 in both entries, the tile (c, r) of a block against itself is always listed, and some device fills all 32 slots. `seeds`: values of 64 or more mark a document without a seed label.
All inputs are finite; a program needn't handle non-finite values.
Results may differ from a plain program's by a relative error of at most 0.00056.
Values may be sent and summed in bfloat16 or wider, within the bound.
No kernel may reach another device: no remote copies, remote signals or barrier semaphores. Data moves between devices by JAX's collectives and lax.ppermute only.
A program may use at most 64 MiB of HBM per device.

v0:
```python
import jax
import jax.numpy as jnp
from jax import lax
from jax.sharding import PartitionSpec as P

CLASSES = 64
ITERS = 3
BLEND = 0.8
EPSILON = 1e-06


def slot_table(picks, slot_alive, extent):
    hits = picks[None, :] == jnp.arange(extent, dtype=jnp.int32)[:, None]
    return (hits & slot_alive[None, :]).astype(jnp.float32)


def settle(to_rows, to_cols, col_index):
    col_share = lax.psum_scatter(to_cols, "row", scatter_dimension=0, tiled=True)
    own_block = lax.dynamic_slice_in_dim(to_rows, col_index, 1, 0) + col_share
    placed = lax.dynamic_update_slice_in_dim(to_rows, own_block, col_index, 0)
    return lax.psum(placed, "col")


def local(embeddings, tile_list, seeds):
    row_index = lax.axis_index("row")
    col_index = lax.axis_index("col")
    row_devices = lax.axis_size("row")
    col_devices = lax.axis_size("col")
    row_count, feat_width = embeddings.shape
    sharpness = feat_width**0.5
    highest = lax.Precision.HIGHEST
    features = embeddings.astype(jnp.float32)
    normed = (
        features * lax.rsqrt(jnp.sum(features * features, axis=1, keepdims=True) + EPSILON)
    ).astype(jnp.bfloat16)
    normed_rows = lax.all_gather(normed, "col", axis=0, tiled=True).reshape(
        col_devices, row_count, feat_width
    )
    normed_cols = lax.all_gather(normed, "row", axis=0, tiled=True).reshape(
        row_devices, row_count, feat_width
    )
    slot_pairs = tile_list.reshape(-1, 2)
    slot_total = slot_pairs.shape[0]
    slot_alive = slot_pairs[:, 0] >= 0
    row_pick = jnp.maximum(slot_pairs[:, 0], 0)
    col_pick = jnp.maximum(slot_pairs[:, 1], 0)
    slot_count = jnp.sum(slot_alive.astype(jnp.int32))
    diagonal = jnp.eye(row_count, dtype=bool)

    def build_group(group_index, kernels):
        offset = group_index * 8
        rows_now = lax.dynamic_slice_in_dim(row_pick, offset, 8)
        cols_now = lax.dynamic_slice_in_dim(col_pick, offset, 8)
        alive_now = lax.dynamic_slice_in_dim(slot_alive, offset, 8)
        scores = jnp.einsum(
            "sie,sje->sij",
            normed_rows[rows_now],
            normed_cols[cols_now],
            preferred_element_type=jnp.float32,
        )
        kernel = jnp.exp(sharpness * (scores - 1.0))
        self_pair = (rows_now == col_index) & (cols_now == row_index)
        masked = self_pair[:, None, None] & diagonal[None] | ~alive_now[:, None, None]
        kernel = jnp.where(masked, 0.0, kernel)
        return lax.dynamic_update_slice_in_dim(kernels, kernel, offset, 0)

    kernels = lax.fori_loop(
        0,
        (slot_count + 7) // 8,
        build_group,
        jnp.zeros((slot_total, row_count, row_count), jnp.float32),
    )
    row_table = slot_table(row_pick, slot_alive, col_devices)
    col_table = slot_table(col_pick, slot_alive, row_devices)
    degree = settle(
        jnp.dot(row_table, jnp.sum(kernels, axis=2), precision=highest),
        jnp.dot(col_table, jnp.sum(kernels, axis=1), precision=highest),
        col_index,
    )
    weight = lax.rsqrt(degree)[:, :, None]
    seeded = (seeds[:, None] == jnp.arange(CLASSES, dtype=jnp.int32)[None, :]).astype(jnp.float32)
    seeded = lax.all_gather(seeded, "col", axis=0, tiled=True).reshape(
        col_devices, row_count, CLASSES
    )
    labels = seeded
    for sweep in range(ITERS):
        spread = weight * labels
        own_spread = lax.dynamic_index_in_dim(spread, col_index, 0, keepdims=False)
        col_labels = lax.all_gather(own_spread, "row", axis=0, tiled=True).reshape(
            row_devices, row_count, CLASSES
        )
        to_rows = jnp.einsum("sij,sjc->sic", kernels, col_labels[col_pick], precision=highest)
        to_cols = jnp.einsum("sij,sic->sjc", kernels, spread[row_pick], precision=highest)
        summed = settle(
            jnp.einsum("as,sic->aic", row_table, to_rows, precision=highest),
            jnp.einsum("bs,sjc->bjc", col_table, to_cols, precision=highest),
            col_index,
        )
        labels = BLEND * weight * summed + (1.0 - BLEND) * seeded
    labels = lax.dynamic_index_in_dim(labels, col_index, 0, keepdims=False)
    return CLASSES * labels


def solution(mesh):
    return jax.shard_map(
        local,
        mesh=mesh,
        in_specs=(P(("row", "col"), None), P("row", "col", None, None), P(("row", "col"))),
        out_specs=P(("row", "col"), None),
        check_vma=False,
    )
```

profile of v0, /device:TPU:2, one launch (start us, length us, event | category | flops | bytes accessed | tf_op | source)
XLA Modules:
  0.0 957.5 jit_solution(11870929973664269903)
XLA Ops:
  6.5 1.1 fusion.18
  7.6 1.7 fusion.19
  10.2 1.3 convert_reduce_fusion
  12.8 58.1 %all_gather.20 = f32[2048,64]{0,1:T(8,128)S(1)} all-gather(f32[128,64]{0,1:T(8,128)S(1)} %fusion.21), channel_id=1, replica_groups=mesh['row'=16,'col'=16] {'col'}, dimensions={0}, use_global_device_ids=true | all-gather | bytes 557056 | tf_op jit(solution)/shard_map/all_gather | solution.py:82
  71.7 10.6 %all-gather.6.cloned.1.call-done = bf16[2048,768]{1,0:T(8,128)(2,1)} async-done(((bf16[128,768]{1,0:T(8,128)(2,1)}), bf16[2048,768]{1,0:T(8,128)(2,1)}) %all-gather.6.cloned.1.call-update) | async-done | bytes 3145744 | tf_op jit(solution)/shard_map/all_gather | solution.py:36
  82.3 37.9 %all-gather.8.cloned.1.call-done = bf16[2048,768]{1,0:T(8,128)(2,1)} async-done(((bf16[128,768]{1,0:T(8,128)(2,1)}), bf16[2048,768]{1,0:T(8,128)(2,1)}) %all-gather.8.cloned.1.call-update) | async-done | bytes 3145744 | tf_op jit(solution)/shard_map/all_gather | solution.py:39
  120.4 40.6 %while.13 = (s32[]{:T(128)}, f32[32,128,128]{2,1,0:T(8,128)S(1)}, s32[]{:T(128)}, s32[32]{0:T(128)S(1)}, s32[]{:T(128)}, /*index=5*/s32[32]{0:T(128)S(1)}, s32[]...) while((s32[]{:T(128)}, f32[32,128,128]{2,1,0:T(8,128)S(1)}, ...), condition=%wide.region_3.4_spmd.clone, body=%wide.region_2.3_spmd.clone.sunk | while | flops 202000464 | bytes 10003999 | solution.py:67
  120.6 3.7 gather_fusion
  124.3 3.8 gather_fusion.1
  128.1 2.5 fusion.81
  130.8 3.7 gather_fusion
  134.5 3.8 gather_fusion.1
  138.2 2.5 fusion.81
  140.9 3.7 gather_fusion
  144.6 3.8 gather_fusion.1
  148.4 2.5 fusion.81
  151.1 3.7 gather_fusion
  154.7 3.8 gather_fusion.1
  158.5 2.5 fusion.81
  161.8 24.1 %all-reduce = f32[16,128]{1,0:T(8,128)S(1)} all-reduce(f32[16,128]{1,0:T(8,128)S(1)} %fusion.28), channel_id=5, replica_groups=mesh['row'=16,'col'=16] {'row'}, use_global_device_ids=true, to_apply=%region_6.7.clone | all-reduce | flops 2048 | bytes 16384
  186.7 45.6 %psum.28 = f32[16,128]{1,0:T(8,128)S(1)} all-reduce(f32[16,128]{1,0:T(8,128)S(1)} %dynamic_update_slice.18), channel_id=1, replica_groups=mesh['row'=16,'col'=16] {'col'}, use_global_device_ids=true, to_apply=%region_7.8 | all-reduce | flops 2048 | bytes 16384 | tf_op jit(solution)/shard_map/psum | solution.py:21
  232.4 0.8 copy-done.1
  233.4 1.6 gather_fusion.3
  235.0 3.2 fusion.55
  238.2 1.1 fusion.14
  239.3 0.9 copy.14
  240.3 1.0 constant_dynamic-slice_fusion.3
  241.3 21.8 %all-gather = f32[1,2048,64]{1,0,2:T(1,128)S(1)} all-gather(f32[1,128,64]{1,0,2:T(1,128)S(1)} %constant_dynamic-slice_fusion.3), channel_id=2, replica_groups=mesh['row'=16,'col'=16] {'row'}, dimensions={1}, use_global_device_ids=true | all-gather | bytes 557056 | tf_op jit(solution)/shard_map/all_gather | solution.py:89
  263.2 1.6 gather_fusion.2
  264.8 5.4 fusion.54
  270.2 1.1 fusion.16
  271.3 28.0 %reduce-scatter.4.cloned.1.call-done = f32[1,128,64]{1,2,0:T(8,128)} async-done(((f32[16,128,64]{1,2,0:T(8,128)}), f32[1,128,64]{1,2,0:T(8,128)}) %reduce-scatter.4.cloned.1.call-update) | async-done | bytes 32784 | tf_op jit(solution)/shard_map/reduce_scatter | solution.py:18
  299.2 0.8 dynamic-slice_add_fusion.3
  301.2 168.8 %all-reduce.5.cloned.1.call-done = f32[16,128,64]{1,0,2:T(8,128)} async-done(((f32[16,128,64]{1,0,2:T(8,128)}), f32[16,128,64]{1,0,2:T(8,128)}) %all-reduce.5.cloned.1.call-update) | async-done | bytes 524304 | tf_op jit(solution)/shard_map/psum | solution.py:21
  470.0 1.1 add_multiply_fusion.1
  471.2 0.8 copy-done
  472.1 1.6 gather_fusion.5
  473.7 3.2 fusion.57
  476.9 1.1 fusion.10
  478.0 0.9 copy.20
  479.0 1.0 constant_dynamic-slice_fusion.2
  480.0 17.9 %all-gather.1 = f32[1,2048,64]{1,0,2:T(1,128)S(1)} all-gather(f32[1,128,64]{1,0,2:T(1,128)S(1)} %constant_dynamic-slice_fusion.2), channel_id=3, replica_groups=mesh['row'=16,'col'=16] {'row'}, dimensions={1}, use_global_device_ids=true | all-gather | bytes 557056 | tf_op jit(solution)/shard_map/all_gather | solution.py:89
  498.1 1.6 gather_fusion.4
  499.6 5.4 fusion.56
  505.0 1.1 fusion.12
  506.1 31.8 %reduce-scatter.6.cloned.1.call-done = f32[1,128,64]{1,2,0:T(8,128)} async-done(((f32[16,128,64]{1,2,0:T(8,128)}), f32[1,128,64]{1,2,0:T(8,128)}) %reduce-scatter.6.cloned.1.call-update) | async-done | bytes 32784 | tf_op jit(solution)/shard_map/reduce_scatter | solution.py:18
  537.9 0.8 dynamic-slice_add_fusion.2
  538.8 0.8 copy-done.5
  539.7 169.3 %all-reduce.7.cloned.1.call-done = f32[16,128,64]{1,0,2:T(8,128)} async-done(((f32[16,128,64]{1,0,2:T(8,128)}), f32[16,128,64]{1,0,2:T(8,128)}) %all-reduce.7.cloned.1.call-update) | async-done | bytes 524304 | tf_op jit(solution)/shard_map/psum | solution.py:21
  709.0 1.9 add_multiply_fusion
  711.0 0.8 copy-done.2
  711.9 1.6 gather_fusion.7
  713.5 3.2 fusion.59
  716.7 1.1 fusion.6
  717.8 1.0 copy.26
  718.8 1.0 constant_dynamic-slice_fusion.1
  719.8 18.1 %all-gather.2 = f32[1,2048,64]{1,0,2:T(1,128)S(1)} all-gather(f32[1,128,64]{1,0,2:T(1,128)S(1)} %constant_dynamic-slice_fusion.1), channel_id=4, replica_groups=mesh['row'=16,'col'=16] {'row'}, dimensions={1}, use_global_device_ids=true | all-gather | bytes 557056 | tf_op jit(solution)/shard_map/all_gather | solution.py:89
  738.1 1.6 gather_fusion.6
  739.7 5.4 fusion.58
  745.0 1.1 fusion.8
  746.1 31.6 %reduce-scatter.8.cloned.1.call-done = f32[1,128,64]{1,2,0:T(8,128)} async-done(((f32[16,128,64]{1,2,0:T(8,128)}), f32[1,128,64]{1,2,0:T(8,128)}) %reduce-scatter.8.cloned.1.call-update) | async-done | bytes 32784 | tf_op jit(solution)/shard_map/reduce_scatter | solution.py:18
  777.7 0.8 dynamic-slice_add_fusion.1
  779.5 169.5 %all-reduce.9.cloned.1.call-done = f32[16,128,64]{1,0,2:T(8,128)} async-done(((f32[16,128,64]{1,0,2:T(8,128)}), f32[16,128,64]{1,0,2:T(8,128)}) %all-reduce.9.cloned.1.call-update) | async-done | bytes 524304 | tf_op jit(solution)/shard_map/psum | solution.py:21
  948.9 1.7 fusion.20
  (74 shorter events, 8.4 us)
Async XLA Ops:
  6.5 64.5 %copy-start.7 = (u32[256]{0:T(256)S(1)}, u32[256]{0:T(256)}, u32[]{:S(2)}) copy-start(u32[256]{0:T(256)} %constant.99) | copy-start | bytes 3076
  6.5 65.2 %copy-start.6 = (s32[1,1,32,2]{2,3,1,0:T(2,128)S(1)}, s32[1,1,32,2]{2,3,1,0:T(2,128)}, u32[]{:S(2)}) copy-start(s32[1,1,32,2]{2,3,1,0:T(2,128)} %param.6) | copy-start | bytes 772
  6.5 75.7 %all-gather.6.cloned.1.call-start = ((), (), s32[]{:S(2)}) async-start(), calls=%async_computation.3 | async-start | bytes 3342336 | tf_op jit(solution)/shard_map/all_gather | solution.py:36
  9.4 110.8 %all-gather.8.cloned.1.call-start = ((), (), s32[]{:S(2)}) async-start(), calls=%async_computation.4 | async-start | bytes 3342336 | tf_op jit(solution)/shard_map/all_gather | solution.py:39
  10.1 289.1 %reduce-scatter.4.cloned.1.call-start = ((), (), s32[]{:S(2)}) async-start(), calls=%async_computation.5 | async-start | bytes 557056 | tf_op jit(solution)/shard_map/reduce_scatter | solution.py:18
  232.4 0.8 copy-start.1
  240.2 229.8 %all-reduce.5.cloned.1.call-start = ((), (), s32[]{:S(2)}) async-start(), calls=%async_computation.6 | async-start | bytes 1048576 | tf_op jit(solution)/shard_map/psum | solution.py:21
  300.2 0.8 copy-start.4
  301.0 236.9 %reduce-scatter.6.cloned.1.call-start = ((), (), s32[]{:S(2)}) async-start(), calls=%async_computation.7 | async-start | bytes 557056 | tf_op jit(solution)/shard_map/reduce_scatter | solution.py:18
  471.2 0.8 copy-start
  478.9 230.1 %all-reduce.7.cloned.1.call-start = ((), (), s32[]{:S(2)}) async-start(), calls=%async_computation.8 | async-start | bytes 1048576 | tf_op jit(solution)/shard_map/psum | solution.py:21
  538.8 0.8 copy-start.5
  539.6 238.1 %reduce-scatter.8.cloned.1.call-start = ((), (), s32[]{:S(2)}) async-start(), calls=%async_computation.9 | async-start | bytes 557056 | tf_op jit(solution)/shard_map/reduce_scatter | solution.py:18
  711.0 0.8 copy-start.2
  718.7 230.2 %all-reduce.9.cloned.1.call-start = ((), (), s32[]{:S(2)}) async-start(), calls=%async_computation.10 | async-start | bytes 1048576 | tf_op jit(solution)/shard_map/psum | solution.py:21
  778.7 0.8 copy-start.3
Sparse Core Ops, SparseCore 0:
  9.8 72.4 all-gather.5
  84.1 36.0 all-gather.7
  240.3 58.8 reduce-scatter.3
  301.7 168.3 all-reduce.4
  479.1 58.7 reduce-scatter.5
  540.4 168.6 all-reduce.6
  718.9 58.7 reduce-scatter.7
  780.3 168.5 all-reduce.8
where the time goes:
time: 959 us; the launch traced here: 957 us
  waiting for transfers between devices  648 us (68%)
  blocking collectives  186 us (19%)
  local copies, waits for them, and re-layouts  52.3 us (5%)
  matrix products  42.2 us (4%)
  between operations  14.5 us (2%)
  other arithmetic  14.1 us (1%)
    psum x3, waiting for transfers between devices, settle(): return lax.psum(placed, 'col')  508 us
    reduce_scatter x3, waiting for transfers between devices, settle(): lax.psum_scatter(to_cols, 'row', scatter_dimension=0, tiled=True)  91.3 us
    all_gather x1, blocking collectives, local(): lax.all_gather(seeded, 'col', axis=0, tiled=True)  58.1 us
    all_gather x3, blocking collectives, local(): lax.all_gather(own_spread, 'row', axis=0, tiled=True)  57.8 us
    psum x1, blocking collectives, settle(): return lax.psum(placed, 'col')  45.6 us
    all_gather x1, waiting for transfers between devices, local(): lax.all_gather(normed, 'row', axis=0, tiled=True)  37.9 us
    unnamed x1, blocking collectives  24.1 us
  transfers between devices with their start and end apart: 8, of which 8 were waited for; matrix products, arithmetic and copies ran while one was open for 3% of the time, Pallas kernels for 0%

commit v1 on v0

--- a/solution.py
+++ b/solution.py
@@ -9,6 +9,12 @@
 EPSILON = 1e-06
 
 
+def summed_here(x, mesh_axis):
+    terms = lax.all_gather(x, mesh_axis, axis=0, tiled=False)
+    summed = terms.sum(axis=0)
+    return summed
+
+
 def slot_table(picks, slot_alive, extent):
     hits = picks[None, :] == jnp.arange(extent, dtype=jnp.int32)[:, None]
     return (hits & slot_alive[None, :]).astype(jnp.float32)
@@ -18,7 +24,7 @@
     col_share = lax.psum_scatter(to_cols, "row", scatter_dimension=0, tiled=True)
     own_block = lax.dynamic_slice_in_dim(to_rows, col_index, 1, 0) + col_share
     placed = lax.dynamic_update_slice_in_dim(to_rows, own_block, col_index, 0)
-    return lax.psum(placed, "col")
+    return summed_here(placed, "col")
 
 
 def local(embeddings, tile_list, seeds):

time: 959 us -> 821 us (0.86); the launches traced: 957 us -> 805 us
  waiting for transfers between devices: 648 us -> 457 us
  blocking collectives: 186 us -> 214 us
  other arithmetic: 14.1 us -> 29.6 us
    psum x3 -> x0, waiting for transfers between devices: 508 us -> none  [settle(): return lax.psum(placed, 'col')]
    all_gather x0 -> x3, waiting for transfers between devices: none -> 317 us  [summed_here(): terms = lax.all_gather(x, mesh_axis, axis=0, tiled=False)]
    psum x1 -> x0, blocking collectives: 45.6 us -> none  [settle(): return lax.psum(placed, 'col')]
    all_gather x0 -> x1, blocking collectives: none -> 44.7 us  [summed_here(): terms = lax.all_gather(x, mesh_axis, axis=0, tiled=False)]
    all_gather x3, blocking collectives: 57.8 us -> 86.3 us  [local(): lax.all_gather(own_spread, 'row', axis=0, tiled=True)]
    reduce_sum x0 -> x4, other arithmetic: none -> 14.4 us  [summed_here(): summed = terms.sum(axis=0)]
  transfers between devices with their start and end apart: 8 -> 8, of which waited for: 8 -> 8; matrix products, arithmetic and copies ran while one was open for 3% -> 4% of each run, Pallas kernels for 0% -> 0%
where the time goes in v1:
time: 821 us; the launch traced here: 805 us
  waiting for transfers between devices  457 us (56%)
  blocking collectives  214 us (26%)
  local copies, waits for them, and re-layouts  48.3 us (6%)
  matrix products  42.2 us (5%)
  other arithmetic  29.6 us (4%)
  between operations  14.4 us (2%)
    all_gather x3, waiting for transfers between devices, summed_here(): terms = lax.all_gather(x, mesh_axis, axis=0, tiled=False)  317 us
    reduce_scatter x3, waiting for transfers between devices, settle(): lax.psum_scatter(to_cols, 'row', scatter_dimension=0, tiled=True)  92 us
    all_gather x3, blocking collectives, local(): lax.all_gather(own_spread, 'row', axis=0, tiled=True)  86.3 us
    all_gather x1, blocking collectives, local(): lax.all_gather(seeded, 'col', axis=0, tiled=True)  58.5 us
    all_gather x1, blocking collectives, summed_here(): terms = lax.all_gather(x, mesh_axis, axis=0, tiled=False)  44.7 us
    all_gather x1, waiting for transfers between devices, local(): lax.all_gather(normed, 'row', axis=0, tiled=True)  38.8 us
    unnamed x1, blocking collectives  24.1 us
  transfers between devices with their start and end apart: 8, of which 8 were waited for; matrix products, arithmetic and copies ran while one was open for 4% of the time, Pallas kernels for 0%

profile of v1, /device:TPU:2, one launch (start us, length us, event | category | flops | bytes accessed | tf_op | source)
XLA Modules:
  0.0 805.5 jit_solution(1998639542384619762)
XLA Ops:
  6.5 1.0 fusion.18
  7.6 1.7 fusion.19
  10.1 1.3 convert_reduce_fusion
  12.1 1.3 dynamic-slice
  15.6 58.5 %all_gather.55 = f32[2048,64]{0,1:T(8,128)S(1)} all-gather(f32[128,64]{0,1:T(8,128)S(1)} %fusion.22), channel_id=1, replica_groups=mesh['row'=16,'col'=16] {'col'}, dimensions={0}, use_global_device_ids=true | all-gather | bytes 557056 | tf_op jit(solution)/shard_map/all_gather | solution.py:88
  74.1 7.9 all-gather.9.cloned.1.call-done
  82.0 38.8 %all-gather.11.cloned.1.call-done = bf16[2048,768]{1,0:T(8,128)(2,1)} async-done(((bf16[128,768]{1,0:T(8,128)(2,1)}), bf16[2048,768]{1,0:T(8,128)(2,1)}) %all-gather.11.cloned.1.call-update) | async-done | bytes 3145744 | tf_op jit(solution)/shard_map/all_gather | solution.py:45
  121.0 40.6 %while.13 = (s32[]{:T(128)}, f32[32,128,128]{2,1,0:T(8,128)S(1)}, s32[]{:T(128)}, s32[32]{0:T(128)S(1)}, s32[]{:T(128)}, /*index=5*/s32[32]{0:T(128)S(1)}, s32[]...) while((s32[]{:T(128)}, f32[32,128,128]{2,1,0:T(8,128)S(1)}, ...), condition=%wide.region_3.4_spmd.clone, body=%wide.region_2.3_spmd.clone.sunk | while | flops 202000464 | bytes 10003999 | solution.py:73
  121.2 3.7 gather_fusion
  124.9 3.8 gather_fusion.1
  128.7 2.5 fusion.86
  131.4 3.7 gather_fusion
  135.1 3.8 gather_fusion.1
  138.8 2.5 fusion.86
  141.5 3.7 gather_fusion
  145.2 3.8 gather_fusion.1
  149.0 2.5 fusion.86
  151.7 3.7 gather_fusion
  155.4 3.8 gather_fusion.1
  159.1 2.5 fusion.86
  162.4 24.1 %all-reduce = f32[16,128]{1,0:T(8,128)S(1)} all-reduce(f32[16,128]{1,0:T(8,128)S(1)} %fusion.29), channel_id=5, replica_groups=mesh['row'=16,'col'=16] {'row'}, use_global_device_ids=true, to_apply=%region_6.7.clone | all-reduce | flops 2048 | bytes 16384
  187.3 44.7 %all_gather.54 = f32[16,16,128]{2,1,0:T(8,128)S(1)} all-gather(f32[1,16,128]{2,1,0:T(8,128)S(1)} %dynamic_update_slice.22), channel_id=1, replica_groups=mesh['row'=16,'col'=16] {'col'}, dimensions={0}, use_global_device_ids=true | all-gather | bytes 139264 | tf_op jit(solution)/shard_map/all_gather | solution.py:13
  232.1 1.6 gather_fusion.3
  233.7 3.2 fusion.57
  236.9 1.1 fusion.14
  238.0 1.0 copy.28
  239.1 21.8 %all-gather = f32[1,2048,64]{1,2,0:T(8,128)S(1)} all-gather(f32[1,128,64]{1,2,0:T(8,128)S(1)} %constant_dynamic-slice_fusion.3), channel_id=2, replica_groups=mesh['row'=16,'col'=16] {'row'}, dimensions={1}, use_global_device_ids=true | all-gather | bytes 557056 | tf_op jit(solution)/shard_map/all_gather | solution.py:95
  261.1 1.6 gather_fusion.2
  262.7 5.4 fusion.56
  268.1 1.1 fusion.16
  269.2 28.6 %reduce-scatter.4.cloned.1.call-done = f32[1,128,64]{1,2,0:T(8,128)} async-done(((f32[16,128,64]{1,2,0:T(8,128)}), f32[1,128,64]{1,2,0:T(8,128)}) %reduce-scatter.4.cloned.1.call-update) | async-done | bytes 32784 | tf_op jit(solution)/shard_map/reduce_scatter | solution.py:24
  297.7 0.8 add_bitcast_fusion.2
  298.7 1.0 copy.31
  299.9 105.5 %all-gather.13.cloned.1.call-done = f32[16,16,128,64]{2,3,1,0:T(8,128)} async-done(((f32[1,16,128,64]{2,3,1,0:T(8,128)}), f32[16,16,128,64]{2,3,1,0:T(8,128)}) %all-gather.13.cloned.1.call-update) | async-done | bytes 8388624 | tf_op jit(solution)/shard_map/all_gather | solution.py:13
  405.4 5.1 reduce_sum.77
  410.5 1.1 add_multiply_fusion.1
  411.6 1.6 gather_fusion.5
  413.2 3.2 fusion.59
  416.4 1.1 fusion.10
  417.5 1.0 copy.38
  418.6 32.3 %all-gather.1 = f32[1,2048,64]{1,2,0:T(8,128)S(1)} all-gather(f32[1,128,64]{1,2,0:T(8,128)S(1)} %constant_dynamic-slice_fusion.2), channel_id=3, replica_groups=mesh['row'=16,'col'=16] {'row'}, dimensions={1}, use_global_device_ids=true | all-gather | bytes 557056 | tf_op jit(solution)/shard_map/all_gather | solution.py:95
  451.1 1.6 gather_fusion.4
  452.7 5.4 fusion.58
  458.1 1.1 fusion.12
  459.2 31.7 %reduce-scatter.6.cloned.1.call-done = f32[1,128,64]{1,2,0:T(8,128)} async-done(((f32[16,128,64]{1,2,0:T(8,128)}), f32[1,128,64]{1,2,0:T(8,128)}) %reduce-scatter.6.cloned.1.call-update) | async-done | bytes 32784 | tf_op jit(solution)/shard_map/reduce_scatter | solution.py:24
  490.9 0.8 add_bitcast_fusion.1
  491.8 1.0 copy.41
  493.1 105.6 %all-gather.15.cloned.1.call-done = f32[16,16,128,64]{2,3,1,0:T(8,128)} async-done(((f32[1,16,128,64]{2,3,1,0:T(8,128)}), f32[16,16,128,64]{2,3,1,0:T(8,128)}) %all-gather.15.cloned.1.call-update) | async-done | bytes 8388624 | tf_op jit(solution)/shard_map/all_gather | solution.py:13
  598.7 5.1 reduce_sum.78
  603.8 2.0 add_multiply_fusion
  605.8 1.6 gather_fusion.7
  607.4 3.2 fusion.61
  610.6 1.1 fusion.6
  611.7 1.0 copy.47
  612.7 32.3 %all-gather.2 = f32[1,2048,64]{1,2,0:T(8,128)S(1)} all-gather(f32[1,128,64]{1,2,0:T(8,128)S(1)} %constant_dynamic-slice_fusion.1), channel_id=4, replica_groups=mesh['row'=16,'col'=16] {'row'}, dimensions={1}, use_global_device_ids=true | all-gather | bytes 557056 | tf_op jit(solution)/shard_map/all_gather | solution.py:95
  645.3 1.6 gather_fusion.6
  646.9 5.4 fusion.60
  652.3 1.1 fusion.8
  653.3 31.7 %reduce-scatter.8.cloned.1.call-done = f32[1,128,64]{1,2,0:T(8,128)} async-done(((f32[16,128,64]{1,2,0:T(8,128)}), f32[1,128,64]{1,2,0:T(8,128)}) %reduce-scatter.8.cloned.1.call-update) | async-done | bytes 32784 | tf_op jit(solution)/shard_map/reduce_scatter | solution.py:24
  685.0 0.8 add_bitcast_fusion
  686.0 1.0 copy.50
  687.1 106.0 %all-gather.17.cloned.1.call-done = f32[16,16,128,64]{2,3,1,0:T(8,128)} async-done(((f32[1,16,128,64]{2,3,1,0:T(8,128)}), f32[16,16,128,64]{2,3,1,0:T(8,128)}) %all-gather.17.cloned.1.call-update) | async-done | bytes 8388624 | tf_op jit(solution)/shard_map/all_gather | solution.py:13
  793.0 4.2 reduce_sum.79
  797.3 1.4 fusion.21
  (64 shorter events, 7.6 us)
Async XLA Ops:
  6.5 75.5 %all-gather.9.cloned.1.call-start = ((), (), s32[]{:S(2)}) async-start(), calls=%async_computation.3 | async-start | bytes 3342336 | tf_op jit(solution)/shard_map/all_gather | solution.py:42
  9.3 111.5 %all-gather.11.cloned.1.call-start = ((), (), s32[]{:S(2)}) async-start(), calls=%async_computation.4 | async-start | bytes 3342336 | tf_op jit(solution)/shard_map/all_gather | solution.py:45
  10.1 287.7 %reduce-scatter.4.cloned.1.call-start = ((), (), s32[]{:S(2)}) async-start(), calls=%async_computation.5 | async-start | bytes 557056 | tf_op jit(solution)/shard_map/reduce_scatter | solution.py:24
  239.0 166.5 %all-gather.13.cloned.1.call-start = ((), (), s32[]{:S(2)}) async-start(), calls=%async_computation.6 | async-start | bytes 8912896 | tf_op jit(solution)/shard_map/all_gather | solution.py:13
  299.7 191.2 %reduce-scatter.6.cloned.1.call-start = ((), (), s32[]{:S(2)}) async-start(), calls=%async_computation.7 | async-start | bytes 557056 | tf_op jit(solution)/shard_map/reduce_scatter | solution.py:24
  418.5 180.2 %all-gather.15.cloned.1.call-start = ((), (), s32[]{:S(2)}) async-start(), calls=%async_computation.8 | async-start | bytes 8912896 | tf_op jit(solution)/shard_map/all_gather | solution.py:13
  492.9 192.2 %reduce-scatter.8.cloned.1.call-start = ((), (), s32[]{:S(2)}) async-start(), calls=%async_computation.9 | async-start | bytes 557056 | tf_op jit(solution)/shard_map/reduce_scatter | solution.py:24
  612.7 180.4 %all-gather.17.cloned.1.call-start = ((), (), s32[]{:S(2)}) async-start(), calls=%async_computation.10 | async-start | bytes 8912896 | tf_op jit(solution)/shard_map/all_gather | solution.py:13
Sparse Core Ops, SparseCore 0:
  9.8 72.1 all-gather.8
  83.8 36.9 all-gather.10
  239.1 58.5 reduce-scatter.3
  300.0 105.3 all-gather.12
  418.6 72.2 reduce-scatter.5
  493.2 105.5 all-gather.14
  612.8 72.2 reduce-scatter.7
  687.5 105.5 all-gather.16
